TPU v7x, 32 devices: a whole 2x2x4 slice. The times are simulated.
32 devices in a mesh: groups: 2 (over y), ctx: 4 (over z), head: 2 (over x), rep: 2 (over core).
Axes of the slice: x: 2, y: 2, z: 4, core: 2. Of those that a mesh axis runs over, the one named last changes fastest.
Arguments:
- hidden: bfloat16 [4096, 7168], P(('groups', 'ctx'), ('head', 'rep')), parts along dimension 0, may hold values from -6 to 6
- kv_down: bfloat16 [7168, 576], P(('head', 'rep')), may hold values from -0.0625 to 0.0625
- kv_gain: float32 [512], replicated, may hold values from 0.1 to 1.9
- queries: bfloat16 [16, 8, 192], P(('groups', 'rep'), ('ctx', 'head')), parts along dimension 0, may hold values from -512 to 512, as said below
- absorb_key: bfloat16 [8, 128, 512], P(('ctx', 'head')), may hold values from -0.5 to 0.5
- absorb_value: bfloat16 [8, 512, 128], P(('ctx', 'head')), may hold values from -0.75 to 0.75
- out_weight: bfloat16 [1024, 7168], P(('ctx', 'head')), may hold values from -0.1875 to 0.1875
- lengths: int32 [16], P(('groups', 'rep')), parts along dimension 0, may hold values from 512 to 2048
Outputs:
- layer_out: bfloat16 [16, 7168], P(('groups', 'rep'), ('ctx', 'head')), parts along dimension 0
There are 2 independent parts, one for each index of `groups`. A program takes and returns all parts, laid end to end along the dimension named above; an argument that names none is the same for every part. Nothing has to cross between parts.
Inputs may be any that keep to these rules, and one draw needn't show every extreme that they name: Continuation b sees the first lengths[b] prompt positions. `queries`: entries are clipped normal values, of order one on most continuations; all query entries of one continuation may be scaled together by a common factor of at most 80.
All inputs are finite; a program needn't handle non-finite values.
Results may differ from a plain program's by a relative error of at most 0.025.
The roundings to bfloat16 on the way count: a program that leaves them out, or rounds other values in their place, can miss the bound.
Values may be sent and summed in bfloat16 or wider, within the bound.
A program may use at most 64 MiB of HBM per device.

v0:
```python
import jax
import jax.numpy as jnp
from jax import lax
from jax.sharding import PartitionSpec as P


def rotate(vectors, position):
    half_width = vectors.shape[-1] // 2
    frequency = 10000.0 ** (-jnp.arange(half_width, dtype=jnp.float32) / half_width)
    angles = position.astype(jnp.float32)[..., None] * frequency
    first_half = vectors[..., :half_width]
    second_half = vectors[..., half_width:]
    return jnp.concatenate(
        [
            first_half * jnp.cos(angles) - second_half * jnp.sin(angles),
            first_half * jnp.sin(angles) + second_half * jnp.cos(angles),
        ],
        -1,
    )


def finish_rows(latent, kv_gain, first_row):
    rank_width = kv_gain.shape[0]
    compressed = latent[:, :rank_width]
    normed = (
        compressed
        * lax.rsqrt(jnp.mean(compressed * compressed, -1, keepdims=True) + 1e-06)
        * kv_gain
    )
    positions = first_row + jnp.arange(latent.shape[0], dtype=jnp.int32)
    return jnp.concatenate([normed, rotate(latent[:, rank_width:], positions)], -1).astype(
        jnp.bfloat16
    )


def shards(hidden, kv_down, kv_gain, queries, absorb_key, absorb_value, out_weight, lengths):
    tok_rows = hidden.shape[0]
    rank_width = kv_gain.shape[0]
    nope_width = absorb_key.shape[1]
    heads_dev = queries.shape[1]
    first_row = lax.axis_index("ctx") * tok_rows
    partial_value = jnp.dot(hidden, kv_down, preferred_element_type=jnp.float32)
    whole_latent = lax.psum(partial_value, ("head", "rep"))
    kv_cache = finish_rows(whole_latent, kv_gain, first_row)
    q_latent = jnp.einsum(
        "bhn,hnr->bhr", queries[..., :nope_width], absorb_key, preferred_element_type=jnp.float32
    )
    q_rotary = rotate(queries[..., nope_width:].astype(jnp.float32), lengths[:, None])
    softmax_scale = queries.shape[2] ** (-0.5)
    qcat = (jnp.concatenate([q_latent, q_rotary], -1) * softmax_scale).astype(jnp.bfloat16)
    gathered = lax.all_gather(qcat, "ctx", axis=1, tiled=True)
    cont_rows = gathered.shape[0]
    head_rows = gathered.shape[1]
    flat_queries = gathered.reshape(cont_rows * head_rows, gathered.shape[2])
    scores = jnp.dot(flat_queries, kv_cache.T, preferred_element_type=jnp.float32).reshape(
        cont_rows, head_rows, tok_rows
    )
    positions = first_row + jnp.arange(tok_rows, dtype=jnp.int32)
    visible = positions[None, None, :] < lengths[:, None, None]
    masked = jnp.where(visible, scores, -1e30)
    row_max = jnp.max(masked, -1)
    weights = jnp.where(visible, jnp.exp(masked - row_max[..., None]), 0.0)
    denominator = jnp.sum(weights, -1)
    flat_weights = weights.astype(jnp.bfloat16).reshape(cont_rows * head_rows, tok_rows)
    context = jnp.dot(
        flat_weights, kv_cache[:, :rank_width], preferred_element_type=jnp.float32
    ).reshape(cont_rows, head_rows, rank_width)
    top_peak = lax.pmax(row_max, "ctx")
    factor = jnp.exp(row_max - top_peak)
    total_own, context_own = (
        lax.psum_scatter(
            (denominator * factor).astype(jnp.bfloat16), "ctx", scatter_dimension=1, tiled=True
        ).astype(jnp.float32),
        lax.psum_scatter(
            (context * factor[..., None]).astype(jnp.bfloat16),
            "ctx",
            scatter_dimension=1,
            tiled=True,
        ).astype(jnp.float32),
    )
    attended = (context_own / total_own[..., None]).astype(jnp.bfloat16)
    head_values = jnp.einsum(
        "bhr,hrv->bhv", attended, absorb_value, preferred_element_type=jnp.float32
    ).astype(jnp.bfloat16)
    flat_values = head_values.reshape(cont_rows, heads_dev * head_values.shape[2])
    out_partial = jnp.dot(flat_values, out_weight, preferred_element_type=jnp.float32)
    return lax.psum_scatter(out_partial, ("ctx", "head"), scatter_dimension=1, tiled=True).astype(
        jnp.bfloat16
    )


def solution(mesh):
    return jax.shard_map(
        shards,
        mesh=mesh,
        in_specs=(
            P(("groups", "ctx"), ("head", "rep")),
            P(("head", "rep"), None),
            P(),
            P(("groups", "rep"), ("ctx", "head"), None),
            P(("ctx", "head"), None, None),
            P(("ctx", "head"), None, None),
            P(("ctx", "head"), None),
            P(("groups", "rep")),
        ),
        out_specs=P(("groups", "rep"), ("ctx", "head")),
        check_vma=False,
    )
```

profile of v0, /device:TPU:0, one launch (start us, length us, event | category | flops | bytes accessed | tf_op | source)
XLA Modules:
  0.0 177.9 jit_solution(9804915051457054022)
XLA Ops:
  6.5 0.0 copy-start
  6.5 0.0 copy-start.7
  6.5 0.0 copy-start.6
  6.5 0.0 copy-start.5
  6.5 0.0 copy-start.3
  6.5 0.0 all-reduce.5.cloned.1.call-start
  6.6 1.6 copy-done
  8.2 3.8 %fusion.49 = f32[512,576]{0,1:T(8,128)} fusion(bf16[512,1792]{1,0:T(8,128)(2,1)} %param.8, bf16[1792,576]{0,1:T(8,128)(2,1)S(1)} %copy-done), kind=kOutput, calls=%fused_computation.65 | convolution fusion | flops 1056964608 | bytes 5079040 | tf_op jit(solution)/shard_map/dot_general | solution.py:42
  12.0 0.0 copy-start.4
  12.0 0.0 all-reduce.5.cloned.1.call-update
  12.0 0.0 reduce-scatter.4.cloned.1.call-start
  12.1 0.0 copy-done.6
  12.1 0.0 copy-done.5
  12.1 0.1 fusion.37
  12.3 0.0 copy-done.3
  12.3 0.1 convolution_bitcast_fusion.1
  12.4 0.0 copy-done.7
  12.4 0.6 dynamic-slice
  13.0 0.1 fusion.24
  13.1 14.9 %all_gather.3 = bf16[4,4,576]{2,0,1:T(4,128)(2,1)S(1)} all-gather(bf16[4,1,576]{2,0,1:T(4,128)(2,1)S(1)} %fusion.24), channel_id=1, replica_groups=mesh['groups'=2,'ctx'=4,'head'=2,'rep'=2] {'ctx'}, dimensions={1}, use_global_device_ids=true | all-gather | bytes 23040 | tf_op jit(solution)/shard_map/all_gather | solution.py:51
  28.0 0.1 broadcast_compare_fusion
  28.1 24.5 %all-reduce.5.cloned.1.call-done = f32[512,576]{0,1:T(8,128)} async-done(((f32[512,576]{0,1:T(8,128)}), f32[512,576]{0,1:T(8,128)}) %all-reduce.5.cloned.1.call-update) | async-done | bytes 1179664 | tf_op jit(solution)/shard_map/psum | solution.py:43
  52.6 0.0 copy-start.1
  52.6 1.4 multiply_reduce_fusion
  54.0 1.2 fusion.14
  55.2 0.0 copy-done.4
  55.2 0.0 copy-done.1
  55.2 0.0 copy-start.2
  55.3 0.1 multiply_convert_fusion
  55.4 0.3 fusion.48
  55.7 11.7 %pmax.7 = f32[4,4]{1,0:T(4,128)S(1)} all-reduce(f32[4,4]{1,0:T(4,128)S(1)} %get-tuple-element.13), channel_id=1, replica_groups=mesh['groups'=2,'ctx'=4,'head'=2,'rep'=2] {'ctx'}, use_global_device_ids=true, to_apply=%region_3.4 | all-reduce | flops 16 | bytes 128 | tf_op jit(solution)/shard_map/pmax | solution.py:68
  67.4 0.2 fusion.17
  67.6 0.3 fusion
  67.8 0.1 copy.20
  68.0 15.8 %all-reduce.2 = (bf16[4,4,512]{2,0,1:T(4,128)(2,1)S(1)}, bf16[4,4]{0,1:T(4,128)(2,1)S(1)}) all-reduce(bf16[4,4,512]{2,0,1:T(4,128)(2,1)S(1)} %copy.19, bf16[4,4]{0,1:T(4,128)(2,1)S(1)} %copy.20), channel_id=2, replica_groups=mesh['groups'=2,'ctx'=4,'head'=2,'rep'=2] {'ctx'}, use_global_device_ids=true, to_apply=%region_4.5.clone | all-reduce | flops 8208 | bytes 32832
  83.7 0.7 fusion.45
  84.4 0.0 copy-done.2
  84.4 4.8 %convolution_bitcast_fusion = f32[7168,4]{1,0:T(8,128)} fusion(bf16[128,7168]{1,0:T(8,128)(2,1)} %param.14, bf16[1,512,128]{2,1,0:T(8,128)(2,1)S(1)} %copy-done.2, bf16[4,4,512]{2,0,1:T(4,128)(2,1)S(1)} %get-tuple-element.5, u32[]{:T(128)} %bitcast.12, f32[4]{0:T(128)S(1)} %fusion.45), kind=kOutput, calls=%fused_computation | convolution fusion | flops 7870976 | bytes 2085380
  89.2 0.0 reduce-scatter.4.cloned.1.call-update
  89.2 80.1 %reduce-scatter.4.cloned.1.call-done = f32[896,4]{1,0:T(8,128)} async-done(((f32[7168,4]{1,0:T(8,128)}), f32[896,4]{1,0:T(8,128)}) %reduce-scatter.4.cloned.1.call-update) | async-done | bytes 14352
  169.3 1.8 %copy.24 = bf16[4,896]{1,0:T(4,128)(2,1)} copy(f32[4,896]{0,1:T(8,128)} %bitcast.38) | data formatting | bytes 21504
  (8 shorter events, 0.1 us)
Async XLA Ops:
  6.5 1.7 copy-start
  6.5 5.9 %copy-start.7 = (u32[32]{0:T(128)S(1)}, u32[32]{0:T(128)}, u32[]{:S(2)}) copy-start(u32[32]{0:T(128)} %constant.30) | copy-start | bytes 388
  6.5 5.6 %copy-start.6 = (s32[4]{0:T(128)S(1)}, s32[4]{0:T(128)}, u32[]{:S(2)}) copy-start(s32[4]{0:T(128)} %param.15) | copy-start | bytes 52
  6.5 5.6 %copy-start.5 = (bf16[4,1,192]{2,0,1:T(4,128)(2,1)S(1)}, bf16[4,1,192]{2,0,1:T(4,128)(2,1)}, u32[]{:S(2)}) copy-start(bf16[4,1,192]{2,0,1:T(4,128)(2,1)} %param.11) | copy-start | bytes 4612
  6.5 5.7 %copy-start.3 = (bf16[1,128,512]{2,1,0:T(8,128)(2,1)S(1)}, bf16[1,128,512]{2,1,0:T(8,128)(2,1)}, u32[]{:S(2)}) copy-start(bf16[1,128,512]{2,1,0:T(8,128)(2,1)} %param.12) | copy-start | bytes 393220
  6.5 46.0 %all-reduce.5.cloned.1.call-start = ((), (), s32[]{:S(2)}) async-start(), calls=%async_computation.1 | async-start | bytes 2359296 | tf_op jit(solution)/shard_map/psum | solution.py:43
  12.0 43.2 %copy-start.4 = (f32[512]{0:T(512)S(1)}, f32[512]{0:T(512)}, u32[]{:S(2)}) copy-start(f32[512]{0:T(512)} %param.10) | copy-start | bytes 6148
  12.0 157.3 %reduce-scatter.4.cloned.1.call-start = ((), (), s32[]{:S(2)}) async-start(), calls=%async_computation.2 | async-start | bytes 4128768
  52.6 2.7 %copy-start.1 = (f32[512,576]{0,1:T(8,128)S(1)}, f32[512,576]{0,1:T(8,128)}, u32[]{:S(2)}) copy-start(f32[512,576]{0,1:T(8,128)} %all-reduce.5.cloned.1.call-done) | copy-start | bytes 3538948
  55.2 29.1 %copy-start.2 = (bf16[1,512,128]{2,1,0:T(8,128)(2,1)S(1)}, bf16[1,512,128]{2,1,0:T(8,128)(2,1)}, u32[]{:S(2)}) copy-start(bf16[1,512,128]{2,1,0:T(8,128)(2,1)} %param.13) | copy-start | bytes 393220
Sparse Core Ops, SparseCore 0:
  12.2 40.3 all-reduce.4
  89.3 79.9 reduce-scatter.3
where the time goes:
time: 178 us
  waiting for transfers between devices  105 us (59%)
  blocking collectives  42.3 us (24%)
  between operations  13.5 us (8%)
  matrix products  9.29 us (5%)
  local copies, waits for them, and re-layouts  4.15 us (2%)
  other arithmetic  3.9 us (2%)
    unnamed x3, waiting for transfers between devices  80.1 us
    psum x1, waiting for transfers between devices, shards(): whole_latent = lax.psum(partial_value, ('head', 'rep'))  24.5 us
    unnamed x1, blocking collectives  15.8 us
    all_gather x1, blocking collectives, shards(): gathered = lax.all_gather(qcat, 'ctx', axis=1, tiled=True)  14.9 us
    pmax x1, blocking collectives, shards(): top_peak = lax.pmax(row_max, 'ctx')  11.7 us
    unnamed x1, matrix products  4.79 us
    unnamed x18, local copies, waits for them, and re-layouts  4.04 us
    dot_general x1, matrix products, shards(): partial_value = jnp.dot(hidden, kv_down, preferred_element_type=jnp.float32)  3.81 us
  transfers between devices with their start and end apart: 2, of which 2 were waited for; matrix products, arithmetic and copies ran while one was open for 1% of the time, Pallas kernels for 0%

commit v1 on v0

--- a/solution.py
+++ b/solution.py
@@ -1,7 +1,15 @@
+import functools
+
 import jax
 import jax.numpy as jnp
+import numpy as np
 from jax import lax
+from jax.experimental import pallas as pl
+from jax.experimental.pallas import tpu as pltpu
 from jax.sharding import PartitionSpec as P
+
+MESH = pl.DeviceIdType.MESH
+LANES = 128
 
 
 def rotate(vectors, position):
@@ -89,9 +97,358 @@
     )
 
 
+def rotary_table(positions, rope_width):
+    half_width = rope_width // 2
+    frequency = (
+        10000.0 ** (-np.arange(half_width, dtype=np.float32) / np.float32(half_width)).astype(np.float64)
+    ).astype(np.float32)
+    angles = (np.arange(positions, dtype=np.float32)[:, None] * frequency).astype(np.float64)
+    cosine, sine = np.cos(angles), np.sin(angles)
+    return np.concatenate([cosine, cosine, -sine, sine], -1).astype(np.float32)
+
+
+def swap_halves(x):
+    half = x.shape[-1] // 2
+    return jnp.concatenate([x[:, half:], x[:, :half]], -1)
+
+
+def split3(x):
+    first = x.astype(jnp.bfloat16).astype(jnp.float32)
+    second = (x - first).astype(jnp.bfloat16).astype(jnp.float32)
+    return first, second, x - first - second
+
+
+def lane_tile(columns, rows):
+    lane = lax.broadcasted_iota(jnp.int32, (rows, LANES), 1)
+    tile = jnp.zeros((rows, LANES), jnp.float32)
+    for i, column in enumerate(columns):
+        tile = jnp.where(lane == i, column, tile)
+    return tile
+
+
+def fused_kernel(
+    n_ctx, n_head, n_rep,
+    hidden, kv_down, gain, queries, absorb_key, absorb_value, out_weight, lengths, table,
+    out,
+    h_buf, kd_buf, gain_buf, q_buf, ak_buf, av_buf, ow_buf, tab_buf,
+    pc, pr, rc, rr, sc, sr, xc, xr,
+    q_all, o_send, o_recv, y_send, y_recv,
+    load_sem, rep_send, rep_recv, head_send, head_recv,
+    q_ssem, q_rsem, o_ssem, o_rsem, y_ssem, y_rsem,
+):
+    g, c = lax.axis_index("groups"), lax.axis_index("ctx")
+    h, r = lax.axis_index("head"), lax.axis_index("rep")
+    n_all, n_out = n_ctx * n_head * n_rep, n_ctx * n_head
+    me, me_out = (c * n_head + h) * n_rep + r, c * n_head + h
+    tok_rows = hidden.shape[0]
+    rows = tok_rows // (n_head * n_rep)
+    rank = gain_buf.shape[1]
+    conts = queries.shape[0]
+    nope = absorb_key.shape[1]
+    rope = queries.shape[2] - nope
+    width = q_all.shape[2]
+    out_cols = y_send.shape[2]
+    f32, bf16 = jnp.float32, jnp.bfloat16
+
+    def peer(index):
+        return (g, index // (n_head * n_rep), (index // n_rep) % n_head, index % n_rep)
+
+    barrier = pltpu.get_barrier_semaphore()
+    for k in range(1, n_all):
+        pl.semaphore_signal(
+            barrier, inc=1, device_id=peer((me + k) % n_all), device_id_type=MESH
+        )
+
+    loads = {}
+
+    def load(name, source, target):
+        loads[name] = pltpu.make_async_copy(source, target, load_sem.at[len(loads)])
+        loads[name].start()
+
+    head_order = list(range(1, n_head)) + [0]
+
+    def load_hidden(k):
+        for k2 in range(n_rep):
+            block = ((h + k) % n_head) * n_rep + (r + k2) % n_rep
+            load(
+                ("hidden", k, k2),
+                hidden.at[pl.ds(pl.multiple_of(block * rows, 8), rows), :],
+                h_buf.at[k, pl.ds(k2 * rows, rows), :],
+            )
+
+    load_hidden(head_order[0])
+    load("kd", kv_down, kd_buf)
+    load("q", queries, q_buf)
+    load("ak", absorb_key, ak_buf)
+    load("table", table, tab_buf)
+    for k in head_order[1:]:
+        load_hidden(k)
+    load("gain", gain, gain_buf)
+    load("av", absorb_value, av_buf)
+    for k in range(n_out):
+        column = pl.multiple_of(((me_out + k) % n_out) * out_cols, LANES)
+        load(("ow", k), out_weight.at[:, pl.ds(column, out_cols)], ow_buf.at[k])
+
+    def remote(source, target, send_sem, recv_sem, device):
+        return pltpu.make_async_remote_copy(
+            src_ref=source, dst_ref=target, send_sem=send_sem, recv_sem=recv_sem,
+            device_id=device, device_id_type=MESH,
+        )
+
+    copies = []
+
+    def project(k):
+        for k2 in range(n_rep):
+            loads["hidden", k, k2].wait()
+        partial = jnp.dot(h_buf[k], kd_buf[...], preferred_element_type=f32)
+        for k2 in range(n_rep):
+            block = partial[k2 * rows : (k2 + 1) * rows]
+            pc[k, k2] = block[:, :rank]
+            pr[k, k2] = jnp.concatenate([block[: rows // 2, rank:], block[rows // 2 :, rank:]], -1)
+
+    def exchange_rep(k):
+        started = []
+        for k2 in range(1, n_rep):
+            to = (g, c, h, (r + k2) % n_rep)
+            slot = (k * n_rep + k2) * 2
+            for j, (source, target) in enumerate(((pc, rc), (pr, rr))):
+                copy = remote(
+                    source.at[k, k2], target.at[k, k2],
+                    rep_send.at[slot + j], rep_recv.at[slot + j], to,
+                )
+                copy.start()
+                started.append(copy)
+        copies.extend(started)
+        return started
+
+    def sum_rep(k, started):
+        for copy in started:
+            copy.wait_recv()
+        total_c, total_r = pc[k, 0], pr[k, 0]
+        for k2 in range(1, n_rep):
+            total_c, total_r = total_c + rc[k, k2], total_r + rr[k, k2]
+        sc[k], sr[k] = total_c, total_r
+
+    def exchange_head(k):
+        to = (g, c, (h + k) % n_head, r)
+        started = []
+        for j, (source, target) in enumerate(((sc, xc), (sr, xr))):
+            copy = remote(
+                source.at[k], target.at[k], head_send.at[k * 2 + j], head_recv.at[k * 2 + j], to
+            )
+            copy.start()
+            started.append(copy)
+        copies.extend(started)
+        return started
+
+    loads["kd"].wait()
+    first = head_order[0]
+    project(first)
+    pl.semaphore_wait(barrier, n_all - 1)
+    in_flight = {first: exchange_rep(first)}
+
+    for name in ("q", "ak", "table"):
+        loads[name].wait()
+    own_q = q_buf[:, 0, :]
+    q_latent = jnp.dot(own_q[:, :nope], ak_buf[0], preferred_element_type=f32)
+    q_rotary = own_q[:, nope:].astype(f32)
+    angles = jnp.concatenate([tab_buf[pl.ds(lengths[b], 1), :] for b in range(conts)], 0)
+    q_rotary = q_rotary * angles[:, :rope] + swap_halves(q_rotary) * angles[:, rope:]
+    scale = queries.shape[2] ** (-0.5)
+    row = lax.broadcasted_iota(jnp.int32, (conts, LANES), 0)
+    length_rows = jnp.zeros((conts, LANES), jnp.int32)
+    for b in range(conts):
+        length_rows = jnp.where(row == b, lengths[b], length_rows)
+    high = length_rows // 64
+    lane = lax.broadcasted_iota(jnp.int32, (conts, LANES), 1)
+    extra = jnp.where(lane == 0, high, length_rows - high * 64).astype(f32)[:, : width - rank - rope]
+    qcat = jnp.concatenate([q_latent * scale, q_rotary * scale, extra], -1)
+    q_all[0] = qcat.astype(bf16)
+    q_copies = []
+    for k in range(1, n_all):
+        copy = remote(
+            q_all.at[0], q_all.at[k], q_ssem.at[k], q_rsem.at[k], peer((me + k) % n_all)
+        )
+        copy.start()
+        q_copies.append(copy)
+    copies.extend(q_copies)
+
+    sent = []
+    if n_head > 1:
+        sum_rep(first, in_flight[first])
+        sent += exchange_head(first)
+        for k in head_order[1:]:
+            project(k)
+            started = exchange_rep(k)
+            sum_rep(k, started)
+            if k:
+                sent += exchange_head(k)
+    else:
+        sum_rep(first, in_flight[first])
+
+    for copy in q_copies:
+        copy.wait_recv()
+    q_rows = jnp.concatenate([q_all[k].astype(f32) for k in range(n_all)], 0)
+    q_lengths = q_rows[:, rank + rope : rank + rope + 1] * 64.0 + q_rows[
+        :, rank + rope + 1 : rank + rope + 2
+    ]
+    loads["gain"].wait()
+    base = c * tok_rows + (h * n_rep + r) * rows
+    token_table = tab_buf[pl.ds(pl.multiple_of(base, 8), rows), :]
+
+    for copy in sent:
+        copy.wait_recv()
+    latent_c, latent_r = sc[0], sr[0]
+    for k in range(1, n_head):
+        latent_c, latent_r = latent_c + xc[k], latent_r + xr[k]
+    latent_r = jnp.concatenate([latent_r[:, :rope], latent_r[:, rope:]], 0)
+    normed = (
+        latent_c
+        * lax.rsqrt(jnp.mean(latent_c * latent_c, -1, keepdims=True) + 1e-06)
+        * gain_buf[...]
+    )
+    rotary = latent_r * token_table[:, :rope] + swap_halves(latent_r) * token_table[:, rope:]
+    kv_c = normed.astype(bf16)
+    kv = jnp.concatenate(
+        [normed, rotary, jnp.zeros((rows, width - rank - rope), f32)], -1
+    ).astype(bf16)
+    scores = lax.dot_general(
+        q_rows.astype(bf16), kv, (((1,), (1,)), ((), ())), preferred_element_type=f32
+    )
+    n_q = n_all * conts
+    positions = (base + lax.broadcasted_iota(jnp.int32, (n_q, rows), 1)).astype(f32)
+    visible = positions < q_lengths
+    masked = jnp.where(visible, scores, -1e30)
+    row_max = jnp.max(masked, -1, keepdims=True)
+    weights = jnp.where(visible, jnp.exp(masked - row_max), 0.0)
+    total = jnp.sum(weights, -1, keepdims=True)
+    context = jnp.dot(weights.astype(bf16), kv_c, preferred_element_type=f32)
+    stats = lane_tile(split3(row_max) + split3(total), n_q)
+    for k in range(n_all):
+        block = slice(k * conts, (k + 1) * conts)
+        target = o_recv if k == 0 else o_send
+        target[k, :, :rank] = context[block].astype(bf16)
+        target[k, :, rank:] = stats[block].astype(bf16)
+    o_copies = []
+    for k in range(1, n_all):
+        copy = remote(
+            o_send.at[k], o_recv.at[k], o_ssem.at[k], o_rsem.at[k],
+            peer((me + n_all - k) % n_all),
+        )
+        copy.start()
+        o_copies.append(copy)
+    copies.extend(o_copies)
+    loads["av"].wait()
+    for k in range(n_out):
+        loads["ow", k].wait()
+    for copy in o_copies:
+        copy.wait_recv()
+
+    parts, maxima, totals = [], [], []
+    for k in range(n_all):
+        part = o_recv[k].astype(f32)
+        parts.append(part[:, :rank])
+        s = part[:, rank:]
+        maxima.append(s[:, 0:1] + s[:, 1:2] + s[:, 2:3])
+        totals.append(s[:, 3:4] + s[:, 4:5] + s[:, 5:6])
+    top = functools.reduce(jnp.maximum, maxima)
+    factors = [jnp.exp(m - top) for m in maxima]
+    total_own = sum(f * t for f, t in zip(factors, totals))
+    context_own = sum(f * p for f, p in zip(factors, parts))
+    attended = (context_own / total_own).astype(bf16)
+    head_values = jnp.dot(attended, av_buf[0], preferred_element_type=f32).astype(bf16)
+    y_copies = []
+    for k in range(1, n_out):
+        y_send[k] = jnp.dot(head_values, ow_buf[k], preferred_element_type=f32).astype(y_send.dtype)
+        to = (me_out + k) % n_out
+        copy = remote(
+            y_send.at[k], y_recv.at[k], y_ssem.at[k], y_rsem.at[k],
+            (g, to // n_head, to % n_head, r),
+        )
+        copy.start()
+        y_copies.append(copy)
+    copies.extend(y_copies)
+    result = jnp.dot(head_values, ow_buf[0], preferred_element_type=f32)
+    for k in range(1, n_out):
+        y_copies[k - 1].wait_recv()
+        result = result + y_recv[k].astype(f32)
+    out[...] = result.astype(out.dtype)
+    for copy in copies:
+        copy.wait_send()
+
+
+def fused(mesh, hidden, kv_down, kv_gain, queries, absorb_key, absorb_value, out_weight, lengths):
+    n_ctx, n_head, n_rep = (mesh.shape[a] for a in ("ctx", "head", "rep"))
+    n_all, n_out = n_ctx * n_head * n_rep, n_ctx * n_head
+    tok_rows, width_dev = hidden.shape
+    rows = tok_rows // (n_head * n_rep)
+    rank = kv_gain.shape[0]
+    latent_width = kv_down.shape[1]
+    rope = latent_width - rank
+    conts = queries.shape[0]
+    padded = rank + LANES
+    out_cols = out_weight.shape[1] // n_out
+    positions = -(-(n_ctx * tok_rows + 1) // 8) * 8
+    table = jnp.asarray(rotary_table(positions, rope))
+    f32, bf16 = jnp.float32, jnp.bfloat16
+    dma = lambda *shape: pltpu.SemaphoreType.DMA(shape)
+    any_space = pl.BlockSpec(memory_space=pl.ANY)
+    vmem = pltpu.VMEM
+    n_loads = n_head * n_rep + 6 + n_out
+    pair_c, pair_r = (n_head, n_rep, rows, rank), (n_head, n_rep, rows // 2, 2 * rope)
+    return pl.pallas_call(
+        functools.partial(fused_kernel, n_ctx, n_head, n_rep),
+        out_shape=jax.ShapeDtypeStruct((conts, out_cols), bf16),
+        in_specs=[any_space] * 7 + [pl.BlockSpec(memory_space=pltpu.SMEM), any_space],
+        out_specs=pl.BlockSpec(memory_space=vmem),
+        scratch_shapes=[
+            vmem((n_head, n_rep * rows, width_dev), bf16),
+            vmem(kv_down.shape, bf16),
+            vmem((1, rank), f32),
+            vmem(queries.shape, bf16),
+            vmem(absorb_key.shape, bf16),
+            vmem(absorb_value.shape, bf16),
+            vmem((n_out, out_weight.shape[0], out_cols), bf16),
+            vmem(table.shape, f32),
+            vmem(pair_c, f32), vmem(pair_r, f32),
+            vmem(pair_c, f32), vmem(pair_r, f32),
+            vmem(pair_c[:1] + pair_c[2:], f32), vmem(pair_r[:1] + pair_r[2:], f32),
+            vmem(pair_c[:1] + pair_c[2:], f32), vmem(pair_r[:1] + pair_r[2:], f32),
+            vmem((n_all, conts, padded), bf16),
+            vmem((n_all, conts, padded), bf16),
+            vmem((n_all, conts, padded), bf16),
+            vmem((n_out, conts, out_cols), bf16),
+            vmem((n_out, conts, out_cols), bf16),
+            dma(n_loads),
+            dma(n_head * n_rep * 2), dma(n_head * n_rep * 2),
+            dma(n_head * 2), dma(n_head * 2),
+            dma(n_all), dma(n_all), dma(n_all), dma(n_all), dma(n_out), dma(n_out),
+        ],
+        compiler_params=pltpu.CompilerParams(collective_id=0, has_side_effects=True),
+    )(
+        hidden, kv_down, kv_gain.reshape(1, rank), queries, absorb_key, absorb_value,
+        out_weight, lengths, table,
+    )
+
+
+def body(mesh, *arrays):
+    hidden, kv_down, kv_gain, queries, absorb_key, _, out_weight, _ = arrays
+    n_ctx, n_head, n_rep = (mesh.shape[a] for a in ("ctx", "head", "rep"))
+    rope = kv_down.shape[1] - kv_gain.shape[0]
+    whole_tiles = (
+        queries.shape[1] == 1
+        and 2 * rope == LANES
+        and queries.shape[2] - absorb_key.shape[1] == rope
+        and kv_gain.shape[0] % LANES == 0
+        and hidden.shape[0] % (n_head * n_rep * 32) == 0
+        and out_weight.shape[1] % (n_ctx * n_head * LANES) == 0
+    )
+    return fused(mesh, *arrays) if whole_tiles else shards(*arrays)
+
+
 def solution(mesh):
     return jax.shard_map(
-        shards,
+        functools.partial(body, mesh),
         mesh=mesh,
         in_specs=(
             P(("groups", "ctx"), ("head", "rep")),

time: 178 us -> 35.3 us (0.20)
  waiting for transfers between devices: 105 us -> 0 us
  blocking collectives: 42.3 us -> 0 us
  Pallas kernels: 0 us -> 28.4 us
  between operations: 13.5 us -> 0.01 us
  matrix products: 9.29 us -> 0 us
  other arithmetic: 3.9 us -> 0 us
  local copies, waits for them, and re-layouts: 4.15 us -> 6.67 us
    unnamed x3 -> x0, waiting for transfers between devices: 80.1 us -> none
    pallas_call x0 -> x1, Pallas kernels: none -> 28.4 us  [fused(): pl.pallas_call(functools.partial(fused_kernel, n_ctx, n_head, n_rep), out...]
    psum x1 -> x0, waiting for transfers between devices: 24.5 us -> none  [shards(): whole_latent = lax.psum(partial_value, ('head', 'rep'))]
    unnamed x1 -> x0, blocking collectives: 15.8 us -> none
    all_gather x1 -> x0, blocking collectives: 14.9 us -> none  [shards(): gathered = lax.all_gather(qcat, 'ctx', axis=1, tiled=True)]
    pmax x1 -> x0, blocking collectives: 11.7 us -> none  [shards(): top_peak = lax.pmax(row_max, 'ctx')]
    unnamed x1 -> x0, matrix products: 4.79 us -> none
    dot_general x4 -> x0, matrix products: 4.5 us -> none  [the longest x1 3.81 us: shards(): partial_value = jnp.dot(hidden, kv_down, preferred_element_type=jnp.float32)]
  transfers between devices with their start and end apart: 2 -> 0, of which waited for: 2 -> 0; matrix products, arithmetic and copies ran while one was open for 1% -> 0% of each run, Pallas kernels for 0% -> 0%
where the time goes in v1:
time: 35.3 us; the launch traced here: 35.1 us
  Pallas kernels  28.4 us (80%)
  local copies, waits for them, and re-layouts  6.67 us (19%)
    pallas_call x1, Pallas kernels, fused(): pl.pallas_call(functools.partial(fused_kernel, n_ctx, n_head, n_rep), out...  28.4 us
    unnamed x3, local copies, waits for them, and re-layouts  6.67 us

profile of v1, /device:TPU:0, one launch (start us, length us, event | category | flops | bytes accessed | tf_op | source)
XLA Modules:
  0.0 35.1 jit_solution(5510472516367613753)
XLA Ops:
  0.0 1.3 %copy.11.queries = bf16[4,1,192]{2,1,0:T(2,128)(2,1)} copy(bf16[4,1,192]{2,0,1:T(4,128)(2,1)} %param.12) | data formatting | bytes 3072 | tf_op args[3]
  1.3 4.1 %copy.10.kv_down = bf16[1792,576]{1,0:T(8,128)(2,1)} copy(bf16[1792,576]{0,1:T(8,128)(2,1)} %param.10) | data formatting | bytes 4128768 | tf_op args[1]
  5.4 28.4 %shard_map.91 = bf16[4,896]{1,0:T(4,128)(2,1)} custom-call(bf16[512,1792]{1,0:T(8,128)(2,1)} %hidden.1, bf16[1792,576]{1,0:T(8,128)(2,1)} %copy.10.kv_down, f32[1,512]{1,0:T(1,128)} %bitcast.1, bf16[4,1,192]{2,1,0:T(2,128)(2,1)} %copy.11.queries, bf16[1,128,512]{2,1,0:T(8,128)(2,1)} %absorb_key.1, bf16[1,512,128]{2,1,0:T(8,128)(2,1)} %absorb_value.1, ...), custom_call_target="tpu_custom_call" | custom-call | tf_op jit(solution)/shard_map/pallas_call | solution.py:399
  33.8 1.3 %copy.13 = bf16[4,896]{1,0:T(4,128)(2,1)} copy(bf16[4,896]{1,0:T(4,128)(2,1)} %shard_map.91) | data formatting | bytes 14336

commit v2 on v1

--- a/solution.py
+++ b/solution.py
@@ -143,7 +143,7 @@
     tok_rows = hidden.shape[0]
     rows = tok_rows // (n_head * n_rep)
     rank = gain_buf.shape[1]
-    conts = queries.shape[0]
+    conts = queries.shape[1]
     nope = absorb_key.shape[1]
     rope = queries.shape[2] - nope
     width = q_all.shape[2]
@@ -200,7 +200,9 @@
     def project(k):
         for k2 in range(n_rep):
             loads["hidden", k, k2].wait()
-        partial = jnp.dot(h_buf[k], kd_buf[...], preferred_element_type=f32)
+        partial = lax.dot_general(
+            h_buf[k], kd_buf[...], (((1,), (1,)), ((), ())), preferred_element_type=f32
+        )
         for k2 in range(n_rep):
             block = partial[k2 * rows : (k2 + 1) * rows]
             pc[k, k2] = block[:, :rank]
@@ -249,7 +251,7 @@
 
     for name in ("q", "ak", "table"):
         loads[name].wait()
-    own_q = q_buf[:, 0, :]
+    own_q = q_buf[0]
     q_latent = jnp.dot(own_q[:, :nope], ak_buf[0], preferred_element_type=f32)
     q_rotary = own_q[:, nope:].astype(f32)
     angles = jnp.concatenate([tab_buf[pl.ds(lengths[b], 1), :] for b in range(conts)], 0)
@@ -403,9 +405,9 @@
         out_specs=pl.BlockSpec(memory_space=vmem),
         scratch_shapes=[
             vmem((n_head, n_rep * rows, width_dev), bf16),
-            vmem(kv_down.shape, bf16),
+            vmem(kv_down.shape[::-1], bf16),
             vmem((1, rank), f32),
-            vmem(queries.shape, bf16),
+            vmem((1, conts, queries.shape[2]), bf16),
             vmem(absorb_key.shape, bf16),
             vmem(absorb_value.shape, bf16),
             vmem((n_out, out_weight.shape[0], out_cols), bf16),
@@ -426,7 +428,7 @@
         ],
         compiler_params=pltpu.CompilerParams(collective_id=0, has_side_effects=True),
     )(
-        hidden, kv_down, kv_gain.reshape(1, rank), queries, absorb_key, absorb_value,
+        hidden, kv_down.T, kv_gain.reshape(1, rank), queries.swapaxes(0, 1), absorb_key, absorb_value,
         out_weight, lengths, table,
     )
 

time: 35.3 us -> 30 us (0.85)
  local copies, waits for them, and re-layouts: 6.67 us -> 1.29 us
    unnamed x3 -> x1, local copies, waits for them, and re-layouts: 6.67 us -> 1.29 us
where the time goes in v2:
time: 30 us; the launch traced here: 29.8 us
  Pallas kernels  28.5 us (95%)
  local copies, waits for them, and re-layouts  1.29 us (4%)
    pallas_call x1, Pallas kernels, fused(): pl.pallas_call(functools.partial(fused_kernel, n_ctx, n_head, n_rep), out...  28.5 us
    unnamed x1, local copies, waits for them, and re-layouts  1.29 us

profile of v2, /device:TPU:0, one launch (start us, length us, event | category | flops | bytes accessed | tf_op | source)
XLA Modules:
  0.0 29.8 jit_solution(17640634375446651689)
XLA Ops:
  0.0 28.5 %shard_map.91 = bf16[4,896]{1,0:T(4,128)(2,1)} custom-call(bf16[512,1792]{1,0:T(8,128)(2,1)} %hidden.1, bf16[576,1792]{1,0:T(8,128)(2,1)} %bitcast.3, f32[1,512]{1,0:T(1,128)} %bitcast.4, bf16[1,4,192]{2,1,0:T(4,128)(2,1)} %bitcast.5, bf16[1,128,512]{2,1,0:T(8,128)(2,1)} %absorb_key.1, bf16[1,512,128]{2,1,0:T(8,128)(2,1)} %absorb_value.1, ...), custom_call_target="tpu_custom_call" | custom-call | tf_op jit(solution)/shard_map/pallas_call | solution.py:401
  28.5 1.3 %copy.11 = bf16[4,896]{1,0:T(4,128)(2,1)} copy(bf16[4,896]{1,0:T(4,128)(2,1)} %shard_map.91) | data formatting | bytes 14336

commit v3 on v2

--- a/solution.py
+++ b/solution.py
@@ -10,6 +10,8 @@
 
 MESH = pl.DeviceIdType.MESH
 LANES = 128
+CHUNK = 256
+STEP = 64
 
 
 def rotate(vectors, position):
@@ -102,7 +104,7 @@
     frequency = (
         10000.0 ** (-np.arange(half_width, dtype=np.float32) / np.float32(half_width)).astype(np.float64)
     ).astype(np.float32)
-    angles = (np.arange(positions, dtype=np.float32)[:, None] * frequency).astype(np.float64)
+    angles = (positions.astype(np.float32)[:, None] * frequency).astype(np.float64)
     cosine, sine = np.cos(angles), np.sin(angles)
     return np.concatenate([cosine, cosine, -sine, sine], -1).astype(np.float32)
 
@@ -116,6 +118,16 @@
     first = x.astype(jnp.bfloat16).astype(jnp.float32)
     second = (x - first).astype(jnp.bfloat16).astype(jnp.float32)
     return first, second, x - first - second
+
+
+def flip(index, mask):
+    bit = 1
+    flipped = index
+    while bit <= mask:
+        if mask & bit:
+            flipped = flipped + bit * (1 - 2 * ((index // bit) % 2))
+        bit *= 2
+    return flipped
 
 
 def lane_tile(columns, rows):
@@ -127,14 +139,14 @@
 
 
 def fused_kernel(
-    n_ctx, n_head, n_rep,
-    hidden, kv_down, gain, queries, absorb_key, absorb_value, out_weight, lengths, table,
+    n_ctx, n_head, n_rep, n_coarse,
+    hidden, kv_down, gain, queries, absorb_key, absorb_value, out_weight, lengths, table, steps,
     out,
-    h_buf, kd_buf, gain_buf, q_buf, ak_buf, av_buf, ow_buf, tab_buf,
+    h_buf, kd_buf, gain_buf, q_buf, ak_buf, av_buf, ow_buf, tab_buf, steps_buf,
     pc, pr, rc, rr, sc, sr, xc, xr,
     q_all, o_send, o_recv, y_send, y_recv,
     load_sem, rep_send, rep_recv, head_send, head_recv,
-    q_ssem, q_rsem, o_ssem, o_rsem, y_ssem, y_rsem,
+    q_ssem, q_rsem, o_ssem, o_rsem, y_ssem, y_rsem, plane_go, all_go,
 ):
     g, c = lax.axis_index("groups"), lax.axis_index("ctx")
     h, r = lax.axis_index("head"), lax.axis_index("rep")
@@ -149,15 +161,24 @@
     width = q_all.shape[2]
     out_cols = y_send.shape[2]
     f32, bf16 = jnp.float32, jnp.bfloat16
+    base = c * tok_rows + (h * n_rep + r) * rows
+    n_chunks = rank // CHUNK
+    columns = [(j * CHUNK, CHUNK) for j in range(n_chunks)] + [(rank, rope)]
+    n_parts = len(columns)
 
     def peer(index):
         return (g, index // (n_head * n_rep), (index // n_rep) % n_head, index % n_rep)
 
+    def signal(semaphore, device):
+        pl.semaphore_signal(semaphore, inc=1, device_id=device, device_id_type=MESH)
+
+    n_plane = n_head * n_rep
+    member = h * n_rep + r
     barrier = pltpu.get_barrier_semaphore()
-    for k in range(1, n_all):
-        pl.semaphore_signal(
-            barrier, inc=1, device_id=peer((me + k) % n_all), device_id_type=MESH
-        )
+
+    @pl.when(member != 0)
+    def _():
+        signal(barrier, (g, c, 0, 0))
 
     loads = {}
 
@@ -169,25 +190,44 @@
 
     def load_hidden(k):
         for k2 in range(n_rep):
-            block = ((h + k) % n_head) * n_rep + (r + k2) % n_rep
+            block = flip(h, k) * n_rep + flip(r, k2)
             load(
                 ("hidden", k, k2),
                 hidden.at[pl.ds(pl.multiple_of(block * rows, 8), rows), :],
                 h_buf.at[k, pl.ds(k2 * rows, rows), :],
             )
 
-    load_hidden(head_order[0])
-    load("kd", kv_down, kd_buf)
     load("q", queries, q_buf)
     load("ak", absorb_key, ak_buf)
-    load("table", table, tab_buf)
-    for k in head_order[1:]:
-        load_hidden(k)
-    load("gain", gain, gain_buf)
-    load("av", absorb_value, av_buf)
-    for k in range(n_out):
-        column = pl.multiple_of(((me_out + k) % n_out) * out_cols, LANES)
-        load(("ow", k), out_weight.at[:, pl.ds(column, out_cols)], ow_buf.at[k])
+    load("steps", steps, steps_buf)
+    load_hidden(head_order[0])
+    for j, (start, size) in enumerate(columns):
+        load(("kd", j), kv_down.at[pl.ds(start, size), :], kd_buf.at[pl.ds(start, size), :])
+
+    def load_rest():
+        for k in head_order[1:]:
+            load_hidden(k)
+        load("gain", gain, gain_buf)
+        load("table", table.at[pl.ds(pl.multiple_of(base, 8), rows), :], tab_buf)
+        load("av", absorb_value, av_buf)
+        for k in range(n_out):
+            out_start = pl.multiple_of(flip(me_out, k) * out_cols, LANES)
+            load(("ow", k), out_weight.at[:, pl.ds(out_start, out_cols)], ow_buf.at[k])
+
+    @pl.when(member == 0)
+    def _():
+        pl.semaphore_wait(barrier, n_plane - 1)
+        for k in range(1, n_plane):
+            signal(plane_go, (g, c, k // n_rep, k % n_rep))
+
+    @pl.when(member != 0)
+    def _():
+        pl.semaphore_wait(plane_go, 1)
+
+    @pl.when(member == 1)
+    def _():
+        for k in range(1, n_ctx):
+            signal(barrier, (g, flip(c, k), h, r))
 
     def remote(source, target, send_sem, recv_sem, device):
         return pltpu.make_async_remote_copy(
@@ -197,112 +237,152 @@
 
     copies = []
 
-    def project(k):
+    def part_of(compressed, rotary, index, j):
+        return compressed.at[index + (j,)] if j < n_chunks else rotary.at[index]
+
+    def project(k, j):
+        start, size = columns[j]
+        block = lax.dot_general(
+            h_buf[k], kd_buf[start : start + size, :], (((1,), (1,)), ((), ())),
+            preferred_element_type=f32,
+        )
         for k2 in range(n_rep):
-            loads["hidden", k, k2].wait()
-        partial = lax.dot_general(
-            h_buf[k], kd_buf[...], (((1,), (1,)), ((), ())), preferred_element_type=f32
-        )
-        for k2 in range(n_rep):
-            block = partial[k2 * rows : (k2 + 1) * rows]
-            pc[k, k2] = block[:, :rank]
-            pr[k, k2] = jnp.concatenate([block[: rows // 2, rank:], block[rows // 2 :, rank:]], -1)
-
-    def exchange_rep(k):
+            own = block[k2 * rows : (k2 + 1) * rows]
+            if j < n_chunks:
+                pc[k, k2, j] = own
+            else:
+                pr[k, k2] = jnp.concatenate([own[: rows // 2], own[rows // 2 :]], -1)
         started = []
         for k2 in range(1, n_rep):
-            to = (g, c, h, (r + k2) % n_rep)
-            slot = (k * n_rep + k2) * 2
-            for j, (source, target) in enumerate(((pc, rc), (pr, rr))):
-                copy = remote(
-                    source.at[k, k2], target.at[k, k2],
-                    rep_send.at[slot + j], rep_recv.at[slot + j], to,
-                )
-                copy.start()
-                started.append(copy)
-        copies.extend(started)
-        return started
-
-    def sum_rep(k, started):
-        for copy in started:
-            copy.wait_recv()
-        total_c, total_r = pc[k, 0], pr[k, 0]
-        for k2 in range(1, n_rep):
-            total_c, total_r = total_c + rc[k, k2], total_r + rr[k, k2]
-        sc[k], sr[k] = total_c, total_r
-
-    def exchange_head(k):
-        to = (g, c, (h + k) % n_head, r)
-        started = []
-        for j, (source, target) in enumerate(((sc, xc), (sr, xr))):
+            slot = (k * n_rep + k2) * n_parts + j
             copy = remote(
-                source.at[k], target.at[k], head_send.at[k * 2 + j], head_recv.at[k * 2 + j], to
+                part_of(pc, pr, (k, k2), j), part_of(rc, rr, (k, k2), j),
+                rep_send.at[slot], rep_recv.at[slot], (g, c, h, flip(r, k2)),
             )
             copy.start()
             started.append(copy)
         copies.extend(started)
         return started
 
-    loads["kd"].wait()
-    first = head_order[0]
-    project(first)
-    pl.semaphore_wait(barrier, n_all - 1)
-    in_flight = {first: exchange_rep(first)}
-
-    for name in ("q", "ak", "table"):
+    def sum_rep(k, j, started):
+        for copy in started:
+            copy.wait_recv()
+        total = part_of(pc, pr, (k, 0), j)[...]
+        for k2 in range(1, n_rep):
+            total = total + part_of(rc, rr, (k, k2), j)[...]
+        part_of(sc, sr, (k,), j)[...] = total
+
+    def exchange_head(k, j):
+        slot = k * n_parts + j
+        copy = remote(
+            part_of(sc, sr, (k,), j), part_of(xc, xr, (k,), j),
+            head_send.at[slot], head_recv.at[slot], (g, c, flip(h, k), r),
+        )
+        copy.start()
+        copies.append(copy)
+        sent.append(copy)
+
+    for name in ("q", "ak", "steps"):
         loads[name].wait()
     own_q = q_buf[0]
     q_latent = jnp.dot(own_q[:, :nope], ak_buf[0], preferred_element_type=f32)
     q_rotary = own_q[:, nope:].astype(f32)
-    angles = jnp.concatenate([tab_buf[pl.ds(lengths[b], 1), :] for b in range(conts)], 0)
-    q_rotary = q_rotary * angles[:, :rope] + swap_halves(q_rotary) * angles[:, rope:]
+    coarse, fine = (
+        jnp.concatenate([steps_buf[pl.ds(row, 1), :] for row in index], 0)
+        for index in (
+            [lengths[b] // STEP for b in range(conts)],
+            [n_coarse + lengths[b] % STEP for b in range(conts)],
+        )
+    )
+    cosine = coarse[:, :rope] * fine[:, :rope] - coarse[:, rope:] * fine[:, rope:]
+    sine = coarse[:, rope:] * fine[:, :rope] + coarse[:, :rope] * fine[:, rope:]
+    q_rotary = q_rotary * cosine + swap_halves(q_rotary) * sine
     scale = queries.shape[2] ** (-0.5)
     row = lax.broadcasted_iota(jnp.int32, (conts, LANES), 0)
     length_rows = jnp.zeros((conts, LANES), jnp.int32)
     for b in range(conts):
         length_rows = jnp.where(row == b, lengths[b], length_rows)
-    high = length_rows // 64
+    high = length_rows // STEP
     lane = lax.broadcasted_iota(jnp.int32, (conts, LANES), 1)
-    extra = jnp.where(lane == 0, high, length_rows - high * 64).astype(f32)[:, : width - rank - rope]
+    extra = jnp.where(lane == 0, high, length_rows - high * STEP).astype(f32)[:, : width - rank - rope]
     qcat = jnp.concatenate([q_latent * scale, q_rotary * scale, extra], -1)
     q_all[0] = qcat.astype(bf16)
     q_copies = []
-    for k in range(1, n_all):
-        copy = remote(
-            q_all.at[0], q_all.at[k], q_ssem.at[k], q_rsem.at[k], peer((me + k) % n_all)
-        )
+    for k in range(1, n_plane):
+        copy = remote(q_all.at[0], q_all.at[k], q_ssem.at[k], q_rsem.at[k], peer(flip(me, k)))
         copy.start()
         q_copies.append(copy)
     copies.extend(q_copies)
 
+    load_rest()
     sent = []
-    if n_head > 1:
-        sum_rep(first, in_flight[first])
-        sent += exchange_head(first)
-        for k in head_order[1:]:
-            project(k)
-            started = exchange_rep(k)
-            sum_rep(k, started)
-            if k:
-                sent += exchange_head(k)
-    else:
-        sum_rep(first, in_flight[first])
+    pending = []
+
+    def drain():
+        k, j, started = pending.pop(0)
+        sum_rep(k, j, started)
+        if k:
+            exchange_head(k, j)
+
+    for k in head_order[:-1]:
+        for k2 in range(n_rep):
+            loads["hidden", k, k2].wait()
+        for j in range(n_parts):
+            if k == head_order[0]:
+                loads["kd", j].wait()
+            pending.append((k, j, project(k, j)))
+            if len(pending) > 1:
+                drain()
+    while pending:
+        drain()
+    for k2 in range(n_rep):
+        loads["hidden", 0, k2].wait()
+    for j in range(n_parts):
+        pending.append((0, j, project(0, j)))
 
     for copy in q_copies:
         copy.wait_recv()
+
+    @pl.when(member == 1)
+    def _():
+        pl.semaphore_wait(barrier, n_ctx - 1)
+        for k in range(n_plane):
+            if k != 1:
+                signal(all_go, (g, c, k // n_rep, k % n_rep))
+
+    @pl.when(member != 1)
+    def _():
+        pl.semaphore_wait(all_go, 1)
+
+    q_far = []
+    for k in range(n_ctx - 1, 0, -1):
+        copy = remote(
+            q_all.at[pl.ds(0, n_plane)], q_all.at[pl.ds(k * n_plane, n_plane)],
+            q_ssem.at[n_plane + k], q_rsem.at[n_plane + k], (g, flip(c, k), h, r),
+        )
+        copy.start()
+        q_far.append(copy)
+    copies.extend(q_far)
+
+    while pending:
+        drain()
+    for copy in q_far:
+        copy.wait_recv()
     q_rows = jnp.concatenate([q_all[k].astype(f32) for k in range(n_all)], 0)
-    q_lengths = q_rows[:, rank + rope : rank + rope + 1] * 64.0 + q_rows[
+    q_lengths = q_rows[:, rank + rope : rank + rope + 1] * float(STEP) + q_rows[
         :, rank + rope + 1 : rank + rope + 2
     ]
     loads["gain"].wait()
-    base = c * tok_rows + (h * n_rep + r) * rows
-    token_table = tab_buf[pl.ds(pl.multiple_of(base, 8), rows), :]
+    loads["table"].wait()
+    token_table = tab_buf[...]
 
     for copy in sent:
         copy.wait_recv()
-    latent_c, latent_r = sc[0], sr[0]
+    latent_c, latent_r = [sc[0, j] for j in range(n_chunks)], sr[0]
     for k in range(1, n_head):
-        latent_c, latent_r = latent_c + xc[k], latent_r + xr[k]
+        latent_c = [latent_c[j] + xc[k, j] for j in range(n_chunks)]
+        latent_r = latent_r + xr[k]
+    latent_c = jnp.concatenate(latent_c, -1)
     latent_r = jnp.concatenate([latent_r[:, :rope], latent_r[:, rope:]], 0)
     normed = (
         latent_c
@@ -332,10 +412,9 @@
         target[k, :, :rank] = context[block].astype(bf16)
         target[k, :, rank:] = stats[block].astype(bf16)
     o_copies = []
-    for k in range(1, n_all):
+    for k in range(n_all - 1, 0, -1):
         copy = remote(
-            o_send.at[k], o_recv.at[k], o_ssem.at[k], o_rsem.at[k],
-            peer((me + n_all - k) % n_all),
+            o_send.at[k], o_recv.at[k], o_ssem.at[k], o_rsem.at[k], peer(flip(me, k))
         )
         copy.start()
         o_copies.append(copy)
@@ -360,9 +439,9 @@
     attended = (context_own / total_own).astype(bf16)
     head_values = jnp.dot(attended, av_buf[0], preferred_element_type=f32).astype(bf16)
     y_copies = []
-    for k in range(1, n_out):
+    for k in range(n_out - 1, 0, -1):
         y_send[k] = jnp.dot(head_values, ow_buf[k], preferred_element_type=f32).astype(y_send.dtype)
-        to = (me_out + k) % n_out
+        to = flip(me_out, k)
         copy = remote(
             y_send.at[k], y_recv.at[k], y_ssem.at[k], y_rsem.at[k],
             (g, to // n_head, to % n_head, r),
@@ -372,7 +451,7 @@
     copies.extend(y_copies)
     result = jnp.dot(head_values, ow_buf[0], preferred_element_type=f32)
     for k in range(1, n_out):
-        y_copies[k - 1].wait_recv()
+        y_copies[n_out - 1 - k].wait_recv()
         result = result + y_recv[k].astype(f32)
     out[...] = result.astype(out.dtype)
     for copy in copies:
@@ -390,18 +469,24 @@
     conts = queries.shape[0]
     padded = rank + LANES
     out_cols = out_weight.shape[1] // n_out
-    positions = -(-(n_ctx * tok_rows + 1) // 8) * 8
-    table = jnp.asarray(rotary_table(positions, rope))
+    tokens = n_ctx * tok_rows
+    table = jnp.asarray(rotary_table(np.arange(tokens), rope))
+    n_coarse = tokens // STEP + 1
+    step_positions = np.concatenate([np.arange(n_coarse) * STEP, np.arange(STEP)])
+    step_positions = np.pad(step_positions, (0, -len(step_positions) % 8))
+    steps = jnp.asarray(rotary_table(step_positions, rope))
     f32, bf16 = jnp.float32, jnp.bfloat16
     dma = lambda *shape: pltpu.SemaphoreType.DMA(shape)
     any_space = pl.BlockSpec(memory_space=pl.ANY)
     vmem = pltpu.VMEM
-    n_loads = n_head * n_rep + 6 + n_out
-    pair_c, pair_r = (n_head, n_rep, rows, rank), (n_head, n_rep, rows // 2, 2 * rope)
+    n_parts = rank // CHUNK + 1
+    n_loads = n_head * n_rep + n_parts + 6 + n_out
+    pair_c = (n_head, n_rep, rank // CHUNK, rows, CHUNK)
+    pair_r = (n_head, n_rep, rows // 2, 2 * rope)
     return pl.pallas_call(
-        functools.partial(fused_kernel, n_ctx, n_head, n_rep),
+        functools.partial(fused_kernel, n_ctx, n_head, n_rep, n_coarse),
         out_shape=jax.ShapeDtypeStruct((conts, out_cols), bf16),
-        in_specs=[any_space] * 7 + [pl.BlockSpec(memory_space=pltpu.SMEM), any_space],
+        in_specs=[any_space] * 7 + [pl.BlockSpec(memory_space=pltpu.SMEM), any_space, any_space],
         out_specs=pl.BlockSpec(memory_space=vmem),
         scratch_shapes=[
             vmem((n_head, n_rep * rows, width_dev), bf16),
@@ -411,7 +496,8 @@
             vmem(absorb_key.shape, bf16),
             vmem(absorb_value.shape, bf16),
             vmem((n_out, out_weight.shape[0], out_cols), bf16),
-            vmem(table.shape, f32),
+            vmem((rows, 2 * rope), f32),
+            vmem(steps.shape, f32),
             vmem(pair_c, f32), vmem(pair_r, f32),
             vmem(pair_c, f32), vmem(pair_r, f32),
             vmem(pair_c[:1] + pair_c[2:], f32), vmem(pair_r[:1] + pair_r[2:], f32),
@@ -422,14 +508,16 @@
             vmem((n_out, conts, out_cols), bf16),
             vmem((n_out, conts, out_cols), bf16),
             dma(n_loads),
-            dma(n_head * n_rep * 2), dma(n_head * n_rep * 2),
-            dma(n_head * 2), dma(n_head * 2),
-            dma(n_all), dma(n_all), dma(n_all), dma(n_all), dma(n_out), dma(n_out),
+            dma(n_head * n_rep * n_parts), dma(n_head * n_rep * n_parts),
+            dma(n_head * n_parts), dma(n_head * n_parts),
+            dma(n_head * n_rep + n_ctx), dma(n_head * n_rep + n_ctx),
+            dma(n_all), dma(n_all), dma(n_out), dma(n_out),
+            pltpu.SemaphoreType.REGULAR, pltpu.SemaphoreType.REGULAR,
         ],
         compiler_params=pltpu.CompilerParams(collective_id=0, has_side_effects=True),
     )(
         hidden, kv_down.T, kv_gain.reshape(1, rank), queries.swapaxes(0, 1), absorb_key, absorb_value,
-        out_weight, lengths, table,
+        out_weight, lengths, table, steps,
     )
 
 
@@ -437,11 +525,13 @@
     hidden, kv_down, kv_gain, queries, absorb_key, _, out_weight, _ = arrays
     n_ctx, n_head, n_rep = (mesh.shape[a] for a in ("ctx", "head", "rep"))
     rope = kv_down.shape[1] - kv_gain.shape[0]
+    sizes = (n_ctx, n_head, n_rep)
     whole_tiles = (
-        queries.shape[1] == 1
+        all(n > 1 and n & (n - 1) == 0 for n in sizes)
+        and queries.shape[1] == 1
         and 2 * rope == LANES
         and queries.shape[2] - absorb_key.shape[1] == rope
-        and kv_gain.shape[0] % LANES == 0
+        and kv_gain.shape[0] % CHUNK == 0
         and hidden.shape[0] % (n_head * n_rep * 32) == 0
         and out_weight.shape[1] % (n_ctx * n_head * LANES) == 0
     )

time: 30 us -> 28.9 us (0.963)
  Pallas kernels: 28.5 us -> 27.4 us
    pallas_call x1, Pallas kernels: 28.5 us -> 27.4 us  [fused(): pl.pallas_call(functools.partial(fused_kernel, n_ctx, n_head, n_rep, n_co...]
where the time goes in v3:
time: 28.9 us; the launch traced here: 28.7 us
  Pallas kernels  27.4 us (95%)
  local copies, waits for them, and re-layouts  1.29 us (4%)
    pallas_call x1, Pallas kernels, fused(): pl.pallas_call(functools.partial(fused_kernel, n_ctx, n_head, n_rep, n_co...  27.4 us
    unnamed x1, local copies, waits for them, and re-layouts  1.29 us

profile of v3, /device:TPU:0, one launch (start us, length us, event | category | flops | bytes accessed | tf_op | source)
XLA Modules:
  0.0 28.7 jit_solution(16267920279722661369)
XLA Ops:
  0.0 27.4 %shard_map.100 = bf16[4,896]{1,0:T(4,128)(2,1)} custom-call(bf16[512,1792]{1,0:T(8,128)(2,1)} %hidden.1, bf16[576,1792]{1,0:T(8,128)(2,1)} %bitcast.3, f32[1,512]{1,0:T(1,128)} %bitcast.4, bf16[1,4,192]{2,1,0:T(4,128)(2,1)} %bitcast.5, bf16[1,128,512]{2,1,0:T(8,128)(2,1)} %absorb_key.1, bf16[1,512,128]{2,1,0:T(8,128)(2,1)} %absorb_value.1, ...), custom_call_target="tpu_custom_call" | custom-call | tf_op jit(solution)/shard_map/pallas_call | solution.py:486
  27.4 1.3 %copy.12 = bf16[4,896]{1,0:T(4,128)(2,1)} copy(bf16[4,896]{1,0:T(4,128)(2,1)} %shard_map.100) | data formatting | bytes 14336
